TPU v7x, 128 devices: a whole 4x4x4 slice. The times are simulated.
128 devices in a mesh: tiles: 16 (over y, z), lag: 8 (over x, core).
Axes of the slice: x: 4, y: 4, z: 4, core: 2. Of those that a mesh axis runs over, the one named last changes fastest.
Arguments:
- spectra: bfloat16 [32, 2, 2, 128, 8192], P('tiles', None, None, None, 'lag'), may hold values from -6 to 6
- requests: int32 [16, 6], replicated, may hold values from 0 to 31, as said below
- pairs: int32 [16, 3, 2], P('tiles'), may hold values from 0 to 5, as said below
- counts: int32 [16], P('tiles'), may hold values from 2 to 3, as said below
Outputs:
- stacked_lags: float32 [48, 64, 128, 128], P('tiles', 'lag')
Inputs may be any that keep to these rules, and one draw needn't show every extreme that they name: Block b is held by index b // 2 of tiles; each row of requests names 6 blocks held by 6 different indices. Each row's 3 entries are pairs (i, j) of request slots with i < j that together use every request slot once. The first counts[d] slots of row d are live, the others give zeros; some index has 3.
All inputs are finite; a program needn't handle non-finite values.
Results may differ from a plain program's by a relative error of at most 0.012.
Values may be sent and summed in bfloat16 or wider, within the bound.
A program may use at most 128 MiB of HBM per device.

v0:
```python
import math
import jax
import jax.numpy as jnp
from jax import lax
from jax.sharding import PartitionSpec as P

F = 8192
W = 2
LAGS = 64
FBLK = 128


def phase_table(freq_first, width):
    frequencies = freq_first + jnp.arange(width, dtype=jnp.int32)
    shifts = (jnp.arange(LAGS, dtype=jnp.int32) - LAGS // 2) % F
    phase_index = frequencies[:, None] * shifts[None, :] % F
    angles = phase_index.astype(jnp.float32) * (2.0 * math.pi / F)
    return jnp.concatenate([jnp.cos(angles), -jnp.sin(angles)], axis=0).astype(jnp.bfloat16)


def cross_block(left_part, right_part):
    left_wide = left_part.astype(jnp.float32)
    right_wide = right_part.astype(jnp.float32)
    real_part = jnp.sum(
        left_wide[:, 0, :, None, :] * right_wide[:, 0, None, :, :]
        + left_wide[:, 1, :, None, :] * right_wide[:, 1, None, :, :],
        axis=0,
    )
    imag_part = jnp.sum(
        left_wide[:, 1, :, None, :] * right_wide[:, 0, None, :, :]
        - left_wide[:, 0, :, None, :] * right_wide[:, 1, None, :, :],
        axis=0,
    )
    channels = left_part.shape[2]
    return (
        jnp.concatenate([real_part, imag_part], axis=-1)
        .reshape(channels * channels, -1)
        .astype(jnp.bfloat16)
    )


def band_sum(left_block, right_block, band_first):
    channels = left_block.shape[2]
    block_count = left_block.shape[-1] // FBLK

    def block_step(running, block_index):
        offset = block_index * FBLK
        left_part = lax.dynamic_slice_in_dim(left_block, offset, FBLK, 3)
        right_part = lax.dynamic_slice_in_dim(right_block, offset, FBLK, 3)
        stacked = cross_block(left_part, right_part)
        phases = phase_table(band_first + offset, FBLK)
        return (
            running
            + lax.dot_general(
                phases, stacked, (((0,), (1,)), ((), ())), preferred_element_type=jnp.float32
            ),
            None,
        )

    running = jnp.zeros((LAGS, channels * channels), jnp.float32)
    running, unused = lax.scan(block_step, running, jnp.arange(block_count, dtype=jnp.int32))
    return running


def per_device(spectra, requests, pairs, counts):
    channels = spectra.shape[3]
    own_index = lax.axis_index("tiles")
    wanted = lax.dynamic_index_in_dim(requests, own_index, 0, keepdims=False)
    empty = jnp.zeros((wanted.shape[0],) + spectra.shape[1:], jnp.bfloat16)
    shards = lax.all_gather(spectra, "tiles", axis=0, tiled=True)
    inside = (wanted >= 0) & (wanted < shards.shape[0])
    taken = jnp.take(shards, jnp.clip(wanted, 0, shards.shape[0] - 1), axis=0)
    needed = jnp.where(inside[:, None, None, None, None], taken, empty)
    band_first = lax.axis_index("lag") * spectra.shape[-1]
    norm_factor = 1.0 / math.sqrt(2.0 * W * F)
    live_count = counts[0]
    tile_pairs = pairs[0]
    slot_total = tile_pairs.shape[0]
    terms = []
    for slot_index in range(slot_total):
        left_block = jnp.take(needed, tile_pairs[slot_index, 0], axis=0)
        right_block = jnp.take(needed, tile_pairs[slot_index, 1], axis=0)
        result = band_sum(left_block, right_block, band_first) * norm_factor
        terms.append(jnp.where(slot_index < live_count, result, jnp.zeros_like(result)))
    partial_terms = jnp.stack(terms).reshape(slot_total, LAGS, channels, channels)
    return lax.psum_scatter(
        partial_terms.astype(jnp.bfloat16), "lag", scatter_dimension=1, tiled=True
    ).astype(jnp.float32)


def solution(mesh):
    placed = (P("tiles", None, None, None, "lag"), P(), P("tiles", None, None), P("tiles"))
    return jax.shard_map(
        per_device,
        mesh=mesh,
        in_specs=placed,
        out_specs=P("tiles", "lag", None, None),
        check_vma=False,
    )
```

profile of v0, /device:TPU:1, one launch (start us, length us, event | category | flops | bytes accessed | tf_op | source)
XLA Modules:
  0.0 1019.2 jit_solution(7977212312652234884)
XLA Ops:
  22.7 187.3 %all-gather.2.cloned.1.call-done = bf16[32,2,2,128,1024]{4,3,2,1,0:T(8,128)(2,1)} async-done(((bf16[2,2,2,128,1024]{4,3,2,1,0:T(8,128)(2,1)}), bf16[32,2,2,128,1024]{4,3,2,1,0:T(8,128)(2,1)}) %all-gather.2.cloned.1.call-update) | async-done | bytes 33554448 | tf_op jit(solution)/shard_map/all_gather | solution.py:70
  221.3 236.1 %while.40 = (s32[]{:T(128)}, f32[64,16384]{1,0:T(8,128)}, s32[8]{0:T(128)S(1)}, s32[]{:T(128)}, bf16[2,2,128,1024]{3,2,1,0:T(8,128)(2,1)S(1)}, /*index=5*/bf16[2...) while((s32[]{:T(128)}, f32[64,16384]{1,0:T(8,128)}, ...), condition=%wide.region_3.5_spmd.clone, body=%wide.region_0.0_spmd.clone.sunk | while | flops 585442176 | bytes 44893884 | solution.py:61
  222.8 11.7 %add_reduce_fusion.6 = (bf16[128,128,128]{2,1,0:T(8,128)(2,1)S(1)}, bf16[128,128,128]{2,1,0:T(8,128)(2,1)}) fusion(f32[2,128,128]{2,1,0:T(8,128)S(1)} %get-tuple-element.564, f32[2,128,128]{2,1,0:T(8,128)S(1)} %get-tuple-element.566, f32[2,128,128]{2,1,0:T(8,128)S(1)} %get-tuple-element.567, f32[2,128,128]{2,1,0:T(8,128)S(1)} %get-tuple-element.568), kind=kLoop, calls=%fused_computation.3.clone.1 | loop fusion | flops 29360128 | bytes 8912896 | tf_op jit(solution)/shard_map/while/body/eval_jaxpr/reduce_sum | solution.py:24
  251.3 11.7 %add_reduce_fusion.6 = (bf16[128,128,128]{2,1,0:T(8,128)(2,1)S(1)}, bf16[128,128,128]{2,1,0:T(8,128)(2,1)}) fusion(f32[2,128,128]{2,1,0:T(8,128)S(1)} %get-tuple-element.564, f32[2,128,128]{2,1,0:T(8,128)S(1)} %get-tuple-element.566, f32[2,128,128]{2,1,0:T(8,128)S(1)} %get-tuple-element.567, f32[2,128,128]{2,1,0:T(8,128)S(1)} %get-tuple-element.568), kind=kLoop, calls=%fused_computation.3.clone.1 | loop fusion | flops 29360128 | bytes 8912896 | tf_op jit(solution)/shard_map/while/body/eval_jaxpr/reduce_sum | solution.py:24
  280.9 11.7 %add_reduce_fusion.6 = (bf16[128,128,128]{2,1,0:T(8,128)(2,1)S(1)}, bf16[128,128,128]{2,1,0:T(8,128)(2,1)}) fusion(f32[2,128,128]{2,1,0:T(8,128)S(1)} %get-tuple-element.564, f32[2,128,128]{2,1,0:T(8,128)S(1)} %get-tuple-element.566, f32[2,128,128]{2,1,0:T(8,128)S(1)} %get-tuple-element.567, f32[2,128,128]{2,1,0:T(8,128)S(1)} %get-tuple-element.568), kind=kLoop, calls=%fused_computation.3.clone.1 | loop fusion | flops 29360128 | bytes 8912896 | tf_op jit(solution)/shard_map/while/body/eval_jaxpr/reduce_sum | solution.py:24
  310.6 11.7 %add_reduce_fusion.6 = (bf16[128,128,128]{2,1,0:T(8,128)(2,1)S(1)}, bf16[128,128,128]{2,1,0:T(8,128)(2,1)}) fusion(f32[2,128,128]{2,1,0:T(8,128)S(1)} %get-tuple-element.564, f32[2,128,128]{2,1,0:T(8,128)S(1)} %get-tuple-element.566, f32[2,128,128]{2,1,0:T(8,128)S(1)} %get-tuple-element.567, f32[2,128,128]{2,1,0:T(8,128)S(1)} %get-tuple-element.568), kind=kLoop, calls=%fused_computation.3.clone.1 | loop fusion | flops 29360128 | bytes 8912896 | tf_op jit(solution)/shard_map/while/body/eval_jaxpr/reduce_sum | solution.py:24
  340.2 11.7 %add_reduce_fusion.6 = (bf16[128,128,128]{2,1,0:T(8,128)(2,1)S(1)}, bf16[128,128,128]{2,1,0:T(8,128)(2,1)}) fusion(f32[2,128,128]{2,1,0:T(8,128)S(1)} %get-tuple-element.564, f32[2,128,128]{2,1,0:T(8,128)S(1)} %get-tuple-element.566, f32[2,128,128]{2,1,0:T(8,128)S(1)} %get-tuple-element.567, f32[2,128,128]{2,1,0:T(8,128)S(1)} %get-tuple-element.568), kind=kLoop, calls=%fused_computation.3.clone.1 | loop fusion | flops 29360128 | bytes 8912896 | tf_op jit(solution)/shard_map/while/body/eval_jaxpr/reduce_sum | solution.py:24
  369.9 11.7 %add_reduce_fusion.6 = (bf16[128,128,128]{2,1,0:T(8,128)(2,1)S(1)}, bf16[128,128,128]{2,1,0:T(8,128)(2,1)}) fusion(f32[2,128,128]{2,1,0:T(8,128)S(1)} %get-tuple-element.564, f32[2,128,128]{2,1,0:T(8,128)S(1)} %get-tuple-element.566, f32[2,128,128]{2,1,0:T(8,128)S(1)} %get-tuple-element.567, f32[2,128,128]{2,1,0:T(8,128)S(1)} %get-tuple-element.568), kind=kLoop, calls=%fused_computation.3.clone.1 | loop fusion | flops 29360128 | bytes 8912896 | tf_op jit(solution)/shard_map/while/body/eval_jaxpr/reduce_sum | solution.py:24
  399.5 11.7 %add_reduce_fusion.6 = (bf16[128,128,128]{2,1,0:T(8,128)(2,1)S(1)}, bf16[128,128,128]{2,1,0:T(8,128)(2,1)}) fusion(f32[2,128,128]{2,1,0:T(8,128)S(1)} %get-tuple-element.564, f32[2,128,128]{2,1,0:T(8,128)S(1)} %get-tuple-element.566, f32[2,128,128]{2,1,0:T(8,128)S(1)} %get-tuple-element.567, f32[2,128,128]{2,1,0:T(8,128)S(1)} %get-tuple-element.568), kind=kLoop, calls=%fused_computation.3.clone.1 | loop fusion | flops 29360128 | bytes 8912896 | tf_op jit(solution)/shard_map/while/body/eval_jaxpr/reduce_sum | solution.py:24
  429.2 11.7 %add_reduce_fusion.6 = (bf16[128,128,128]{2,1,0:T(8,128)(2,1)S(1)}, bf16[128,128,128]{2,1,0:T(8,128)(2,1)}) fusion(f32[2,128,128]{2,1,0:T(8,128)S(1)} %get-tuple-element.564, f32[2,128,128]{2,1,0:T(8,128)S(1)} %get-tuple-element.566, f32[2,128,128]{2,1,0:T(8,128)S(1)} %get-tuple-element.567, f32[2,128,128]{2,1,0:T(8,128)S(1)} %get-tuple-element.568), kind=kLoop, calls=%fused_computation.3.clone.1 | loop fusion | flops 29360128 | bytes 8912896 | tf_op jit(solution)/shard_map/while/body/eval_jaxpr/reduce_sum | solution.py:24
  460.7 244.2 %while.41 = (s32[]{:T(128)}, f32[64,16384]{1,0:T(8,128)}, s32[8]{0:T(128)S(1)}, s32[]{:T(128)}, bf16[2,2,128,1024]{3,2,1,0:T(8,128)(2,1)}, /*index=5*/bf16[2,2,1...) while((s32[]{:T(128)}, f32[64,16384]{1,0:T(8,128)}, s32[8]{0:T(128)S(1)}, ...), condition=%wide.region_7.9_spmd.clone, body=%wide.region_4.8_spmd.clone.sunk | while | flops 585442176 | bytes 44893884 | solution.py:61
  463.2 11.7 %add_reduce_fusion.7 = (bf16[128,128,128]{2,1,0:T(8,128)(2,1)S(1)}, bf16[128,128,128]{2,1,0:T(8,128)(2,1)}) fusion(f32[2,128,128]{2,1,0:T(8,128)S(1)} %get-tuple-element.580, f32[2,128,128]{2,1,0:T(8,128)S(1)} %get-tuple-element.582, f32[2,128,128]{2,1,0:T(8,128)S(1)} %get-tuple-element.583, f32[2,128,128]{2,1,0:T(8,128)S(1)} %get-tuple-element.584), kind=kLoop, calls=%fused_computation.34.clone.1 | loop fusion | flops 29360128 | bytes 8912896 | tf_op jit(solution)/shard_map/while/body/eval_jaxpr/reduce_sum | solution.py:24
  492.7 11.7 %add_reduce_fusion.7 = (bf16[128,128,128]{2,1,0:T(8,128)(2,1)S(1)}, bf16[128,128,128]{2,1,0:T(8,128)(2,1)}) fusion(f32[2,128,128]{2,1,0:T(8,128)S(1)} %get-tuple-element.580, f32[2,128,128]{2,1,0:T(8,128)S(1)} %get-tuple-element.582, f32[2,128,128]{2,1,0:T(8,128)S(1)} %get-tuple-element.583, f32[2,128,128]{2,1,0:T(8,128)S(1)} %get-tuple-element.584), kind=kLoop, calls=%fused_computation.34.clone.1 | loop fusion | flops 29360128 | bytes 8912896 | tf_op jit(solution)/shard_map/while/body/eval_jaxpr/reduce_sum | solution.py:24
  511.7 9.3 convolution_add_fusion.7
  523.3 11.7 %add_reduce_fusion.7 = (bf16[128,128,128]{2,1,0:T(8,128)(2,1)S(1)}, bf16[128,128,128]{2,1,0:T(8,128)(2,1)}) fusion(f32[2,128,128]{2,1,0:T(8,128)S(1)} %get-tuple-element.580, f32[2,128,128]{2,1,0:T(8,128)S(1)} %get-tuple-element.582, f32[2,128,128]{2,1,0:T(8,128)S(1)} %get-tuple-element.583, f32[2,128,128]{2,1,0:T(8,128)S(1)} %get-tuple-element.584), kind=kLoop, calls=%fused_computation.34.clone.1 | loop fusion | flops 29360128 | bytes 8912896 | tf_op jit(solution)/shard_map/while/body/eval_jaxpr/reduce_sum | solution.py:24
  554.0 11.7 %add_reduce_fusion.7 = (bf16[128,128,128]{2,1,0:T(8,128)(2,1)S(1)}, bf16[128,128,128]{2,1,0:T(8,128)(2,1)}) fusion(f32[2,128,128]{2,1,0:T(8,128)S(1)} %get-tuple-element.580, f32[2,128,128]{2,1,0:T(8,128)S(1)} %get-tuple-element.582, f32[2,128,128]{2,1,0:T(8,128)S(1)} %get-tuple-element.583, f32[2,128,128]{2,1,0:T(8,128)S(1)} %get-tuple-element.584), kind=kLoop, calls=%fused_computation.34.clone.1 | loop fusion | flops 29360128 | bytes 8912896 | tf_op jit(solution)/shard_map/while/body/eval_jaxpr/reduce_sum | solution.py:24
  573.0 9.3 convolution_add_fusion.7
  584.6 11.7 %add_reduce_fusion.7 = (bf16[128,128,128]{2,1,0:T(8,128)(2,1)S(1)}, bf16[128,128,128]{2,1,0:T(8,128)(2,1)}) fusion(f32[2,128,128]{2,1,0:T(8,128)S(1)} %get-tuple-element.580, f32[2,128,128]{2,1,0:T(8,128)S(1)} %get-tuple-element.582, f32[2,128,128]{2,1,0:T(8,128)S(1)} %get-tuple-element.583, f32[2,128,128]{2,1,0:T(8,128)S(1)} %get-tuple-element.584), kind=kLoop, calls=%fused_computation.34.clone.1 | loop fusion | flops 29360128 | bytes 8912896 | tf_op jit(solution)/shard_map/while/body/eval_jaxpr/reduce_sum | solution.py:24
  615.3 11.7 %add_reduce_fusion.7 = (bf16[128,128,128]{2,1,0:T(8,128)(2,1)S(1)}, bf16[128,128,128]{2,1,0:T(8,128)(2,1)}) fusion(f32[2,128,128]{2,1,0:T(8,128)S(1)} %get-tuple-element.580, f32[2,128,128]{2,1,0:T(8,128)S(1)} %get-tuple-element.582, f32[2,128,128]{2,1,0:T(8,128)S(1)} %get-tuple-element.583, f32[2,128,128]{2,1,0:T(8,128)S(1)} %get-tuple-element.584), kind=kLoop, calls=%fused_computation.34.clone.1 | loop fusion | flops 29360128 | bytes 8912896 | tf_op jit(solution)/shard_map/while/body/eval_jaxpr/reduce_sum | solution.py:24
  645.9 11.7 %add_reduce_fusion.7 = (bf16[128,128,128]{2,1,0:T(8,128)(2,1)S(1)}, bf16[128,128,128]{2,1,0:T(8,128)(2,1)}) fusion(f32[2,128,128]{2,1,0:T(8,128)S(1)} %get-tuple-element.580, f32[2,128,128]{2,1,0:T(8,128)S(1)} %get-tuple-element.582, f32[2,128,128]{2,1,0:T(8,128)S(1)} %get-tuple-element.583, f32[2,128,128]{2,1,0:T(8,128)S(1)} %get-tuple-element.584), kind=kLoop, calls=%fused_computation.34.clone.1 | loop fusion | flops 29360128 | bytes 8912896 | tf_op jit(solution)/shard_map/while/body/eval_jaxpr/reduce_sum | solution.py:24
  664.9 9.3 convolution_add_fusion.7
  676.6 11.7 %add_reduce_fusion.7 = (bf16[128,128,128]{2,1,0:T(8,128)(2,1)S(1)}, bf16[128,128,128]{2,1,0:T(8,128)(2,1)}) fusion(f32[2,128,128]{2,1,0:T(8,128)S(1)} %get-tuple-element.580, f32[2,128,128]{2,1,0:T(8,128)S(1)} %get-tuple-element.582, f32[2,128,128]{2,1,0:T(8,128)S(1)} %get-tuple-element.583, f32[2,128,128]{2,1,0:T(8,128)S(1)} %get-tuple-element.584), kind=kLoop, calls=%fused_computation.34.clone.1 | loop fusion | flops 29360128 | bytes 8912896 | tf_op jit(solution)/shard_map/while/body/eval_jaxpr/reduce_sum | solution.py:24
  709.5 243.4 %while.42 = (s32[]{:T(128)}, f32[64,16384]{1,0:T(8,128)}, s32[8]{0:T(128)S(1)}, s32[]{:T(128)}, bf16[2,2,128,1024]{3,2,1,0:T(8,128)(2,1)}, /*index=5*/bf16[2,2,1...) while((s32[]{:T(128)}, f32[64,16384]{1,0:T(8,128)}, s32[8]{0:T(128)S(1)}, ...), condition=%wide.region_11.13_spmd.clone, body=%wide.region_8.12_spmd.clone.sunk | while | flops 585442176 | bytes 44893884 | solution.py:61
  711.9 11.7 %add_reduce_fusion.8 = (bf16[128,128,128]{2,1,0:T(8,128)(2,1)S(1)}, bf16[128,128,128]{2,1,0:T(8,128)(2,1)}) fusion(f32[2,128,128]{2,1,0:T(8,128)S(1)} %get-tuple-element.596, f32[2,128,128]{2,1,0:T(8,128)S(1)} %get-tuple-element.598, f32[2,128,128]{2,1,0:T(8,128)S(1)} %get-tuple-element.599, f32[2,128,128]{2,1,0:T(8,128)S(1)} %get-tuple-element.600), kind=kLoop, calls=%fused_computation.65.clone.1 | loop fusion | flops 29360128 | bytes 8912896 | tf_op jit(solution)/shard_map/while/body/eval_jaxpr/reduce_sum | solution.py:24
  741.3 11.7 %add_reduce_fusion.8 = (bf16[128,128,128]{2,1,0:T(8,128)(2,1)S(1)}, bf16[128,128,128]{2,1,0:T(8,128)(2,1)}) fusion(f32[2,128,128]{2,1,0:T(8,128)S(1)} %get-tuple-element.596, f32[2,128,128]{2,1,0:T(8,128)S(1)} %get-tuple-element.598, f32[2,128,128]{2,1,0:T(8,128)S(1)} %get-tuple-element.599, f32[2,128,128]{2,1,0:T(8,128)S(1)} %get-tuple-element.600), kind=kLoop, calls=%fused_computation.65.clone.1 | loop fusion | flops 29360128 | bytes 8912896 | tf_op jit(solution)/shard_map/while/body/eval_jaxpr/reduce_sum | solution.py:24
  771.9 11.7 %add_reduce_fusion.8 = (bf16[128,128,128]{2,1,0:T(8,128)(2,1)S(1)}, bf16[128,128,128]{2,1,0:T(8,128)(2,1)}) fusion(f32[2,128,128]{2,1,0:T(8,128)S(1)} %get-tuple-element.596, f32[2,128,128]{2,1,0:T(8,128)S(1)} %get-tuple-element.598, f32[2,128,128]{2,1,0:T(8,128)S(1)} %get-tuple-element.599, f32[2,128,128]{2,1,0:T(8,128)S(1)} %get-tuple-element.600), kind=kLoop, calls=%fused_computation.65.clone.1 | loop fusion | flops 29360128 | bytes 8912896 | tf_op jit(solution)/shard_map/while/body/eval_jaxpr/reduce_sum | solution.py:24
  802.4 11.7 %add_reduce_fusion.8 = (bf16[128,128,128]{2,1,0:T(8,128)(2,1)S(1)}, bf16[128,128,128]{2,1,0:T(8,128)(2,1)}) fusion(f32[2,128,128]{2,1,0:T(8,128)S(1)} %get-tuple-element.596, f32[2,128,128]{2,1,0:T(8,128)S(1)} %get-tuple-element.598, f32[2,128,128]{2,1,0:T(8,128)S(1)} %get-tuple-element.599, f32[2,128,128]{2,1,0:T(8,128)S(1)} %get-tuple-element.600), kind=kLoop, calls=%fused_computation.65.clone.1 | loop fusion | flops 29360128 | bytes 8912896 | tf_op jit(solution)/shard_map/while/body/eval_jaxpr/reduce_sum | solution.py:24
  833.0 11.7 %add_reduce_fusion.8 = (bf16[128,128,128]{2,1,0:T(8,128)(2,1)S(1)}, bf16[128,128,128]{2,1,0:T(8,128)(2,1)}) fusion(f32[2,128,128]{2,1,0:T(8,128)S(1)} %get-tuple-element.596, f32[2,128,128]{2,1,0:T(8,128)S(1)} %get-tuple-element.598, f32[2,128,128]{2,1,0:T(8,128)S(1)} %get-tuple-element.599, f32[2,128,128]{2,1,0:T(8,128)S(1)} %get-tuple-element.600), kind=kLoop, calls=%fused_computation.65.clone.1 | loop fusion | flops 29360128 | bytes 8912896 | tf_op jit(solution)/shard_map/while/body/eval_jaxpr/reduce_sum | solution.py:24
  863.6 11.7 %add_reduce_fusion.8 = (bf16[128,128,128]{2,1,0:T(8,128)(2,1)S(1)}, bf16[128,128,128]{2,1,0:T(8,128)(2,1)}) fusion(f32[2,128,128]{2,1,0:T(8,128)S(1)} %get-tuple-element.596, f32[2,128,128]{2,1,0:T(8,128)S(1)} %get-tuple-element.598, f32[2,128,128]{2,1,0:T(8,128)S(1)} %get-tuple-element.599, f32[2,128,128]{2,1,0:T(8,128)S(1)} %get-tuple-element.600), kind=kLoop, calls=%fused_computation.65.clone.1 | loop fusion | flops 29360128 | bytes 8912896 | tf_op jit(solution)/shard_map/while/body/eval_jaxpr/reduce_sum | solution.py:24
  894.1 11.7 %add_reduce_fusion.8 = (bf16[128,128,128]{2,1,0:T(8,128)(2,1)S(1)}, bf16[128,128,128]{2,1,0:T(8,128)(2,1)}) fusion(f32[2,128,128]{2,1,0:T(8,128)S(1)} %get-tuple-element.596, f32[2,128,128]{2,1,0:T(8,128)S(1)} %get-tuple-element.598, f32[2,128,128]{2,1,0:T(8,128)S(1)} %get-tuple-element.599, f32[2,128,128]{2,1,0:T(8,128)S(1)} %get-tuple-element.600), kind=kLoop, calls=%fused_computation.65.clone.1 | loop fusion | flops 29360128 | bytes 8912896 | tf_op jit(solution)/shard_map/while/body/eval_jaxpr/reduce_sum | solution.py:24
  924.7 11.7 %add_reduce_fusion.8 = (bf16[128,128,128]{2,1,0:T(8,128)(2,1)S(1)}, bf16[128,128,128]{2,1,0:T(8,128)(2,1)}) fusion(f32[2,128,128]{2,1,0:T(8,128)S(1)} %get-tuple-element.596, f32[2,128,128]{2,1,0:T(8,128)S(1)} %get-tuple-element.598, f32[2,128,128]{2,1,0:T(8,128)S(1)} %get-tuple-element.599, f32[2,128,128]{2,1,0:T(8,128)S(1)} %get-tuple-element.600), kind=kLoop, calls=%fused_computation.65.clone.1 | loop fusion | flops 29360128 | bytes 8912896 | tf_op jit(solution)/shard_map/while/body/eval_jaxpr/reduce_sum | solution.py:24
  967.2 42.6 %reduce-scatter.5.cloned.1.call-done = bf16[8,49152]{1,0:T(8,128)(2,1)} async-done(((bf16[64,49152]{1,0:T(8,128)(2,1)}), bf16[8,49152]{1,0:T(8,128)(2,1)}) %reduce-scatter.5.cloned.1.call-update) | async-done | bytes 786448
  (293 shorter events, 439.3 us)
Async XLA Ops:
  6.5 203.4 %all-gather.2.cloned.1.call-start = ((), (), s32[]{:S(2)}) async-start(), calls=%async_computation.1 | async-start | bytes 35651584 | tf_op jit(solution)/shard_map/all_gather | solution.py:70
  7.3 1002.5 %reduce-scatter.5.cloned.1.call-start = ((), (), s32[]{:S(2)}) async-start(), calls=%async_computation.2 | async-start | bytes 7077888
  952.9 3.5 copy-start
Sparse Core Ops, SparseCore 0:
  9.5 200.4 all-gather.1
  967.3 42.4 reduce-scatter.4
where the time goes:
time: 1020 us
  other arithmetic  475 us (47%)
  waiting for transfers between devices  231 us (23%)
  matrix products  218 us (21%)
  local copies, waits for them, and re-layouts  53.4 us (5%)
  between operations  25.5 us (2%)
  loops' own time  16.6 us (2%)
    reduce_sum x24, other arithmetic, cross_block(): jnp.sum(left_wide[:, 0, :, None, :] * right_wide[:, 0, None, :, :] + left...  280 us
    dot_general x24, matrix products, block_step(): lax.dot_general(phases, stacked, (((0,), (1,)), ((), ())), preferred_elem...  218 us
    all_gather x1, waiting for transfers between devices, per_device(): shards = lax.all_gather(spectra, 'tiles', axis=0, tiled=True)  187 us
    concatenate x24, other arithmetic, cross_block(): jnp.concatenate([real_part, imag_part], axis=-1)  171 us
    unnamed x3, waiting for transfers between devices  43.3 us
  transfers between devices with their start and end apart: 2, of which 2 were waited for; matrix products, arithmetic and copies ran while one was open for 0% of the time, Pallas kernels for 0%

commit v1 on v0

--- a/solution.py
+++ b/solution.py
@@ -67,7 +67,8 @@
     own_index = lax.axis_index("tiles")
     wanted = lax.dynamic_index_in_dim(requests, own_index, 0, keepdims=False)
     empty = jnp.zeros((wanted.shape[0],) + spectra.shape[1:], jnp.bfloat16)
-    shards = lax.all_gather(spectra, "tiles", axis=0, tiled=True)
+    outgoing = jnp.stack([spectra] * lax.axis_size("tiles"))
+    shards = jnp.concatenate(lax.all_to_all(outgoing, "tiles", 0, 0), axis=0)
     inside = (wanted >= 0) & (wanted < shards.shape[0])
     taken = jnp.take(shards, jnp.clip(wanted, 0, shards.shape[0] - 1), axis=0)
     needed = jnp.where(inside[:, None, None, None, None], taken, empty)

time: 1020 us -> 1460 us (1.43)
  waiting for transfers between devices: 231 us -> 654 us
    all_to_all x0 -> x1, waiting for transfers between devices: none -> 606 us  [per_device(): shards = jnp.concatenate(lax.all_to_all(outgoing, 'tiles', 0, 0), axis=0)]
    all_gather x1 -> x0, waiting for transfers between devices: 187 us -> none  [per_device(): shards = lax.all_gather(spectra, 'tiles', axis=0, tiled=True)]
    unnamed x3 -> x2, waiting for transfers between devices: 43.3 us -> 47.9 us
where the time goes in v1:
time: 1460 us
  waiting for transfers between devices  654 us (45%)
  other arithmetic  473 us (32%)
  matrix products  217 us (15%)
  local copies, waits for them, and re-layouts  63.3 us (4%)
  between operations  25.8 us (2%)
  loops' own time  15 us (1%)
    all_to_all x1, waiting for transfers between devices, per_device(): shards = jnp.concatenate(lax.all_to_all(outgoing, 'tiles', 0, 0), axis=0)  606 us
    reduce_sum x24, other arithmetic, cross_block(): jnp.sum(left_wide[:, 0, :, None, :] * right_wide[:, 0, None, :, :] + left...  280 us
    dot_general x24, matrix products, block_step(): lax.dot_general(phases, stacked, (((0,), (1,)), ((), ())), preferred_elem...  217 us
    concatenate x24, other arithmetic, cross_block(): jnp.concatenate([real_part, imag_part], axis=-1)  170 us
    unnamed x2, waiting for transfers between devices  47.9 us
  transfers between devices with their start and end apart: 2, of which 2 were waited for; matrix products, arithmetic and copies ran while one was open for 0% of the time, Pallas kernels for 0%

profile of v1, /device:TPU:1, one launch (start us, length us, event | category | flops | bytes accessed | tf_op | source)
XLA Modules:
  0.0 1457.1 jit_solution(6158072131427987901)
XLA Ops:
  6.5 12.2 stack.10
  40.9 606.3 %all-to-all-done = bf16[16,2,2,2,128,1024]{5,4,3,2,1,0:T(8,128)(2,1)} async-done(((bf16[16,2,2,2,128,1024]{5,4,3,2,1,0:T(8,128)(2,1)}), bf16[16,2,2,2,128,1024]{5,4,3,2,1,0:T(8,128)(2,1)}, u32[]{:S(2)}, u32[]{:S(2)}) %all-to-all-start) | async-done | bytes 33554464 | tf_op jit(solution)/shard_map/all_to_all | solution.py:71
  658.6 234.8 %while.40 = (s32[]{:T(128)}, f32[64,16384]{1,0:T(8,128)}, s32[8]{0:T(128)S(1)}, s32[]{:T(128)}, bf16[2,2,128,1024]{3,2,1,0:T(8,128)(2,1)S(1)}, /*index=5*/bf16[2...) while((s32[]{:T(128)}, f32[64,16384]{1,0:T(8,128)}, ...), condition=%wide.region_3.5_spmd.clone, body=%wide.region_0.0_spmd.clone.sunk | while | flops 585442176 | bytes 44893884 | solution.py:61
  659.9 11.6 add_reduce_fusion.6
  688.2 11.6 add_reduce_fusion.6
  717.7 11.6 add_reduce_fusion.6
  747.2 11.6 add_reduce_fusion.6
  776.7 11.6 add_reduce_fusion.6
  806.2 11.6 add_reduce_fusion.6
  835.7 11.6 add_reduce_fusion.6
  865.2 11.6 add_reduce_fusion.6
  896.7 241.9 %while.41 = (s32[]{:T(128)}, f32[64,16384]{1,0:T(8,128)}, s32[8]{0:T(128)S(1)}, s32[]{:T(128)}, bf16[2,2,128,1024]{3,2,1,0:T(8,128)(2,1)}, /*index=5*/bf16[2,2,1...) while((s32[]{:T(128)}, f32[64,16384]{1,0:T(8,128)}, s32[8]{0:T(128)S(1)}, ...), condition=%wide.region_7.9_spmd.clone, body=%wide.region_4.8_spmd.clone.sunk | while | flops 585442176 | bytes 44893884 | solution.py:61
  899.1 11.6 add_reduce_fusion.7
  928.3 11.6 add_reduce_fusion.7
  958.6 11.6 add_reduce_fusion.7
  989.0 11.6 add_reduce_fusion.7
  1019.4 11.6 add_reduce_fusion.7
  1049.7 11.6 add_reduce_fusion.7
  1080.1 11.6 add_reduce_fusion.7
  1110.4 11.6 add_reduce_fusion.7
  1143.2 242.3 %while.42 = (s32[]{:T(128)}, f32[64,16384]{1,0:T(8,128)}, s32[8]{0:T(128)S(1)}, s32[]{:T(128)}, bf16[2,2,128,1024]{3,2,1,0:T(8,128)(2,1)}, /*index=5*/bf16[2,2,1...) while((s32[]{:T(128)}, f32[64,16384]{1,0:T(8,128)}, s32[8]{0:T(128)S(1)}, ...), condition=%wide.region_11.13_spmd.clone, body=%wide.region_8.12_spmd.clone.sunk | while | flops 585442176 | bytes 44893884 | solution.py:61
  1145.5 11.6 add_reduce_fusion.8
  1174.7 11.6 add_reduce_fusion.8
  1193.7 9.2 convolution_add_fusion.8
  1205.2 11.6 add_reduce_fusion.8
  1224.2 9.2 convolution_add_fusion.8
  1235.6 11.6 add_reduce_fusion.8
  1266.0 11.6 add_reduce_fusion.8
  1296.5 11.6 add_reduce_fusion.8
  1326.9 11.6 add_reduce_fusion.8
  1357.3 11.6 add_reduce_fusion.8
  1399.8 47.9 %reduce-scatter.5.cloned.1.call-done = bf16[8,49152]{1,0:T(8,128)(2,1)} async-done(((bf16[64,49152]{1,0:T(8,128)(2,1)}), bf16[8,49152]{1,0:T(8,128)(2,1)}) %reduce-scatter.5.cloned.1.call-update) | async-done | bytes 786448
  (297 shorter events, 451.9 us)
Async XLA Ops:
  18.7 8.9 copy-start.2
  18.7 21.8 %copy-start.1 = (s32[16,6]{0,1:T(8,128)S(1)}, s32[16,6]{0,1:T(8,128)}, u32[]{:S(2)}) copy-start(s32[16,6]{0,1:T(8,128)} %param.13) | copy-start | bytes 1156
  18.7 628.5 %all-to-all-start = ((bf16[16,2,2,2,128,1024]{5,4,3,2,1,0:T(8,128)(2,1)}), bf16[16,2,2,2,128,1024]{5,4,3,2,1,0:T(8,128)(2,1)}, u32[]{:S(2)}, u32[]{:S(2)}) async-start(bf16[16,2,2,2,128,1024]{5,4,3,2,1,0:T(8,128)(2,1)} %stack.10), calls=%async_computation | async-start | bytes 67108864 | tf_op jit(solution)/shard_map/all_to_all | solution.py:71
  27.5 1420.1 %reduce-scatter.5.cloned.1.call-start = ((), (), s32[]{:S(2)}) async-start(), calls=%async_computation.2 | async-start | bytes 7077888
  1385.5 3.5 copy-start
Sparse Core Ops, SparseCore 0:
  1399.9 47.7 reduce-scatter.4
